TPU v7x, 32 devices: a whole 2x2x4 slice. The times are simulated.
32 devices in a mesh: groups: 1, expert: 32 (over z, y, x, core).
Axes of the slice: x: 2, y: 2, z: 4, core: 2. Of those that a mesh axis runs over, the one named last changes fastest.
Arguments:
- normed: bfloat16 [256, 7168], P(('groups', 'expert')), may hold values from -6 to 6
- expert_ids: int32 [256, 2], P(('groups', 'expert')), may hold values from 0 to 3, all different within a row; in each aligned block of 8 rows (0 to 7, 8 to 15, ...) at most 5 rows name the same one
- gate_levels: int32 [256, 2], P(('groups', 'expert')), may hold values from 1 to 255
- placement: int32 [32], replicated, may hold values from 0 to 3, as said below
- w_gate: bfloat16 [32, 7168, 256], P('expert'), may hold values from -0.0625 to 0.0625
- w_up: bfloat16 [32, 7168, 256], P('expert'), may hold values from -0.0625 to 0.0625
- w_down: bfloat16 [32, 256, 7168], P('expert'), may hold values from -0.125 to 0.125
- q_latent: bfloat16 [256, 64, 512], P(('groups', 'expert')), may hold values from -48 to 48
- q_rope: bfloat16 [256, 4096], P(('groups', 'expert')), may hold values from -48 to 48
- cache_latent: bfloat16 [256, 64, 512], P(('groups', 'expert')), may hold values from -6 to 6
- cache_rope: bfloat16 [256, 64, 64], P(('groups', 'expert')), may hold values from -6 to 6
- lengths: int32 [256], P(('groups', 'expert')), may hold values from 2 to 64, as said below
Outputs:
- moe_out: bfloat16 [256, 7168], P(('groups', 'expert'))
- attended: bfloat16 [256, 64, 512], P(('groups', 'expert'))
Inputs may be any that keep to these rules, and one draw needn't show every extreme that they name: `expert_ids`: within the rows of one device an expert is named at most 5 times. `placement`: each expert is held by exactly 8 devices. `lengths`: some device holds a request of 64 positions.
All inputs are finite; a program needn't handle non-finite values.
Results may differ from a plain program's by a relative error of at most 0.0085.
Values may be sent and summed in bfloat16 or wider, within the bound.
A program may use at most 128 MiB of HBM per device.

v0:
```python
import jax
import jax.numpy as jnp
from jax import lax
from jax.sharding import PartitionSpec as P

FF = 2048


score_scale = 192.0 ** (-0.5)
route_scale = 2.5


def route_weights(gate_levels):
    levels = gate_levels.astype(jnp.float32)
    return route_scale * levels / jnp.sum(levels, axis=1, keepdims=True)


def expert_block(slot_rows, gate_mat, up_mat, down_mat):
    shape = slot_rows.shape
    flattened = slot_rows.reshape(-1, shape[-1])
    gate_proj = jnp.dot(flattened, gate_mat, preferred_element_type=jnp.float32)
    up_proj = jnp.dot(flattened, up_mat, preferred_element_type=jnp.float32)
    hidden = (jax.nn.silu(gate_proj) * up_proj).astype(jnp.bfloat16)
    partial_value = jnp.dot(hidden, down_mat, preferred_element_type=jnp.float32).astype(
        jnp.bfloat16
    )
    return partial_value.reshape(shape[0], shape[1], down_mat.shape[1])


def latent_attention(q_latent, q_rope, cache_latent, cache_rope, lengths):
    tok_rows, heads = (q_latent.shape[0], q_latent.shape[1])
    rope_query = q_rope.reshape(tok_rows, heads, -1)
    scores = jnp.einsum("bhc,blc->bhl", q_latent, cache_latent, preferred_element_type=jnp.float32)
    scores = scores + jnp.einsum(
        "bhr,brl->bhl", rope_query, cache_rope, preferred_element_type=jnp.float32
    )
    scores = scores * score_scale
    visible = jnp.arange(cache_latent.shape[1])[None, None, :] < lengths[:, None, None]
    scores = jnp.where(visible, scores, jnp.full_like(scores, -1e30))
    top_score = jnp.max(scores, axis=-1, keepdims=True)
    exponent = jnp.where(visible, jnp.exp(scores - top_score), jnp.zeros_like(scores))
    probs = (exponent / jnp.sum(exponent, axis=-1, keepdims=True)).astype(jnp.bfloat16)
    return jnp.einsum(
        "bhl,blc->bhc", probs, cache_latent, preferred_element_type=jnp.float32
    ).astype(jnp.bfloat16)


def per_device(
    normed,
    expert_ids,
    gate_levels,
    placement,
    w_gate,
    w_up,
    w_down,
    q_latent,
    q_rope,
    cache_latent,
    cache_rope,
    lengths,
):
    n_dev = lax.axis_size("expert")
    tok_rows, width = normed.shape
    top_count = expert_ids.shape[1]
    slice_width = w_gate.shape[2]
    experts_all = n_dev * slice_width // FF
    capacity = max(tok_rows * 5 // 8, tok_rows * top_count // experts_all)
    gate_mat = w_gate[0]
    up_mat = w_up[0]
    down_mat = w_down[0]
    expert_range = jnp.arange(experts_all, dtype=jnp.int32)
    slot_range = jnp.arange(capacity, dtype=jnp.int32)
    picked = (expert_ids[:, :, None] == expert_range[None, None, :]).astype(jnp.int32)
    routed = jnp.sum(picked, axis=1)
    slot_index = jnp.cumsum(routed, axis=0) - routed
    token_slot = jnp.sum(picked * slot_index[:, None, :], axis=2)
    holder = (placement[:, None] == expert_range[None, :]).astype(jnp.float32)
    chosen = (
        (routed.T[:, None, :] == 1) & (slot_index.T[:, None, :] == slot_range[None, :, None])
    ).astype(jnp.float32)
    selector = jnp.einsum("de,ect->dct", holder, chosen).astype(jnp.bfloat16)
    outgoing = jnp.einsum(
        "dct,tm->dcm", selector, normed, preferred_element_type=jnp.float32
    ).astype(jnp.bfloat16)
    partials = expert_block(
        lax.all_to_all(outgoing, "expert", split_axis=0, concat_axis=0, tiled=True),
        gate_mat,
        up_mat,
        down_mat,
    )
    returned = lax.all_to_all(partials, "expert", split_axis=0, concat_axis=0, tiled=True)
    collect = (
        (placement[None, None, :, None] == expert_ids[:, :, None, None])
        & (slot_range[None, None, None, :] == token_slot[:, :, None, None])
    ).astype(jnp.bfloat16)
    summed = jnp.einsum("tkdc,dcm->tkm", collect, returned, preferred_element_type=jnp.float32)
    weights = route_weights(gate_levels)
    moe_out = jnp.sum(weights[:, :, None] * summed, axis=1).astype(jnp.bfloat16)
    attended = latent_attention(q_latent, q_rope, cache_latent, cache_rope, lengths)
    return (moe_out, attended)


def solution(mesh):
    in_specs = (
        P(("groups", "expert"), None),
        P(("groups", "expert"), None),
        P(("groups", "expert"), None),
        P(),
        P("expert", None, None),
        P("expert", None, None),
        P("expert", None, None),
        P(("groups", "expert"), None, None),
        P(("groups", "expert"), None),
        P(("groups", "expert"), None, None),
        P(("groups", "expert"), None, None),
        P(("groups", "expert")),
    )
    out_specs = (P(("groups", "expert"), None), P(("groups", "expert"), None, None))
    return jax.shard_map(
        per_device, mesh=mesh, in_specs=in_specs, out_specs=out_specs, check_vma=False
    )
```

profile of v0, /device:TPU:0, one launch (start us, length us, event | category | flops | bytes accessed | tf_op | source)
XLA Modules:
  0.0 203.5 jit_solution(3293159134365110137)
XLA Ops:
  0.6 0.0 copy-start
  0.6 0.8 convert_reduce_fusion
  1.4 0.2 reduce_window_sum.11
  1.6 1.9 convolution_convert_fusion.1
  3.5 1.3 copy.33
  4.8 90.2 %all_to_all.10 = bf16[32,5,7168]{2,1,0:T(8,128)(2,1)} all-to-all(bf16[32,5,7168]{2,1,0:T(8,128)(2,1)S(1)} %copy.33), channel_id=1, replica_groups=mesh['groups'=1,'expert'=32] {'expert'}, dimensions={0} | all-to-all | bytes 4587520 | tf_op jit(solution)/shard_map/all_to_all | solution.py:86
  95.0 3.3 %reshape.64 = bf16[160,7168]{1,0:T(8,128)(2,1)S(1)} reshape(bf16[32,5,7168]{2,1,0:T(8,128)(2,1)} %all_to_all.10) | data formatting | bytes 4587520 | tf_op jit(solution)/shard_map/reshape | solution.py:20
  98.2 2.8 %fusion.5 = f32[160,256]{1,0:T(8,128)S(1)} fusion(bf16[160,7168]{1,0:T(8,128)(2,1)S(1)} %reshape.64, bf16[1,7168,256]{2,1,0:T(8,128)(2,1)} %param.16), kind=kOutput, calls=%fused_computation.8 | convolution fusion | flops 587202560 | bytes 6127616 | tf_op jit(solution)/shard_map/dot_general | solution.py:21
  101.0 7.1 %convolution_convert_fusion = bf16[160,7168]{1,0:T(8,128)(2,1)} fusion(bf16[1,256,7168]{2,1,0:T(8,128)(2,1)} %param.18, bf16[160,7168]{1,0:T(8,128)(2,1)S(1)} %reshape.64, bf16[1,7168,256]{2,1,0:T(8,128)(2,1)} %param.17, f32[160,256]{1,0:T(8,128)S(1)} %fusion.5), kind=kOutput, calls=%fused_computation.1 | convolution fusion | flops 1175797760 | bytes 12091392 | tf_op jit(solution)/shard_map/dot_general | solution.py:24
  108.2 4.6 %reshape.65 = bf16[32,5,7168]{2,1,0:T(8,128)(2,1)} reshape(bf16[160,7168]{1,0:T(8,128)(2,1)} %convolution_convert_fusion) | data formatting | bytes 4587520 | tf_op jit(solution)/shard_map/reshape | solution.py:27
  112.7 0.0 copy-start.3
  112.7 0.0 copy-start.6
  112.7 0.0 copy-start.4
  112.7 0.0 copy-start.7
  112.7 0.0 copy-start.1
  112.8 0.0 copy-start.2
  112.8 0.0 copy-start.5
  112.8 3.7 %all-to-all-start.1 = ((bf16[32,5,7168]{2,1,0:T(8,128)(2,1)}), bf16[32,5,7168]{2,1,0:T(8,128)(2,1)}, u32[]{:S(2)}, u32[]{:S(2)}) async-start(bf16[32,5,7168]{2,1,0:T(8,128)(2,1)} %reshape.65), calls=%async_computation.1 | async-start | bytes 7340032 | tf_op jit(solution)/shard_map/all_to_all | solution.py:91
  116.5 0.0 copy-done.3
  116.5 0.2 reshape.66
  116.7 0.0 copy-done.6
  116.7 0.0 copy-done.4
  116.7 0.0 copy-done.7
  116.7 0.1 iota_compare_fusion.2
  116.8 0.0 copy-done
  116.8 0.0 copy-done.1
  116.8 0.3 fusion.52
  117.1 0.0 copy-done.2
  117.1 0.3 fusion.14
  117.4 0.1 fusion.51
  117.5 0.0 copy-done.5
  117.5 0.1 broadcast_compare_fusion
  117.6 1.3 convolution_convert_fusion.2
  118.9 80.3 %all-to-all-done.1 = bf16[32,5,7168]{2,1,0:T(8,128)(2,1)} async-done(((bf16[32,5,7168]{2,1,0:T(8,128)(2,1)}), bf16[32,5,7168]{2,1,0:T(8,128)(2,1)}, u32[]{:S(2)}, u32[]{:S(2)}) %all-to-all-start.1) | async-done | bytes 2293792 | tf_op jit(solution)/shard_map/all_to_all | solution.py:91
  199.2 4.3 %fusion.10 = bf16[8,7168]{1,0:T(8,128)(2,1)} fusion(bf16[32,5,7168]{2,1,0:T(8,128)(2,1)} %all-to-all-done.1, f32[8,2]{0,1:T(2,128)S(1)} %multiply_divide_fusion, pred[8,2,5]{0,2,1:T(8,128)(4,1)S(1)} %iota_compare_fusion.1, pred[8,2,32]{2,0,1:T(8,128)(4,1)S(1)} %broadcast_compare_fusion), kind=kOutput, calls=%fused_computation.14 | convolution fusion | flops 36874752 | bytes 2409104 | tf_op jit(solution)/shard_map/tkdc,dcm->tkm/dot_general | solution.py:96
  (6 shorter events, 0.1 us)
Async XLA Ops:
  0.6 116.2 %copy-start = (bf16[8,64,512]{2,1,0:T(8,128)(2,1)S(1)}, bf16[8,64,512]{2,1,0:T(8,128)(2,1)}, u32[]{:S(2)}) copy-start(bf16[8,64,512]{2,1,0:T(8,128)(2,1)} %param.21) | copy-start | bytes 1572868
  112.7 3.7 %copy-start.3 = (bf16[8,4096]{1,0:T(8,128)(2,1)S(1)}, bf16[8,4096]{1,0:T(8,128)(2,1)}, u32[]{:S(2)}) copy-start(bf16[8,4096]{1,0:T(8,128)(2,1)} %param.20) | copy-start | bytes 196612
  112.7 3.9 %copy-start.6 = (s32[8,2]{0,1:T(2,128)S(1)}, s32[8,2]{0,1:T(2,128)}, u32[]{:S(2)}) copy-start(s32[8,2]{0,1:T(2,128)} %param.14) | copy-start | bytes 196
  112.7 4.0 %copy-start.4 = (s32[8,2]{0,1:T(2,128)S(1)}, s32[8,2]{0,1:T(2,128)}, u32[]{:S(2)}) copy-start(s32[8,2]{0,1:T(2,128)} %param.13) | copy-start | bytes 196
  112.7 4.0 %copy-start.7 = (s32[8]{0:T(128)S(1)}, s32[8]{0:T(128)}, u32[]{:S(2)}) copy-start(s32[8]{0:T(128)} %param.23) | copy-start | bytes 100
  112.7 4.1 %copy-start.1 = (bf16[8,64,512]{2,1,0:T(8,128)(2,1)S(1)}, bf16[8,64,512]{2,1,0:T(8,128)(2,1)}, u32[]{:S(2)}) copy-start(bf16[8,64,512]{2,1,0:T(8,128)(2,1)} %param.19) | copy-start | bytes 1572868
  112.8 4.3 %copy-start.2 = (bf16[8,64,64]{2,1,0:T(8,128)(2,1)S(1)}, bf16[8,64,64]{2,1,0:T(8,128)(2,1)}, u32[]{:S(2)}) copy-start(bf16[8,64,64]{2,1,0:T(8,128)(2,1)} %param.22) | copy-start | bytes 196612
  112.8 4.8 %copy-start.5 = (s32[32]{0:T(128)S(1)}, s32[32]{0:T(128)}, u32[]{:S(2)}) copy-start(s32[32]{0:T(128)} %param.15) | copy-start | bytes 388
  112.8 86.4 %all-to-all-start.1 = ((bf16[32,5,7168]{2,1,0:T(8,128)(2,1)}), bf16[32,5,7168]{2,1,0:T(8,128)(2,1)}, u32[]{:S(2)}, u32[]{:S(2)}) async-start(bf16[32,5,7168]{2,1,0:T(8,128)(2,1)} %reshape.65), calls=%async_computation.1 | async-start | bytes 7340032 | tf_op jit(solution)/shard_map/all_to_all | solution.py:91
where the time goes:
time: 204 us; the launch traced here: 203 us
  blocking collectives  90.2 us (44%)
  waiting for transfers between devices  80.3 us (39%)
  matrix products  17.9 us (9%)
  local copies, waits for them, and re-layouts  9.32 us (5%)
  starting transfers between devices  3.69 us (2%)
    all_to_all x1, blocking collectives, per_device(): lax.all_to_all(outgoing, 'expert', split_axis=0, concat_axis=0, tiled=True)  90.2 us
    all_to_all x1, waiting for transfers between devices, per_device(): lax.all_to_all(partials, 'expert', split_axis=0, concat_axis=0, tiled=True)  80.3 us
    dot_general x1, matrix products, expert_block(): jnp.dot(hidden, down_mat, preferred_element_type=jnp.float32)  7.15 us
    reshape x1, local copies, waits for them, and re-layouts, expert_block(): return partial_value.reshape(shape[0], shape[1], down_mat.shape[1])  4.55 us
    dot_general x1, matrix products, per_device(): jnp.einsum('tkdc,dcm->tkm', collect, returned, preferred_element_type=jnp...  4.28 us
  transfers between devices with their start and end apart: 1, of which 1 were waited for; matrix products, arithmetic and copies ran while one was open for 1% of the time, Pallas kernels for 0%

commit v1 on v0

v1 whole, which is shorter than its diff:
```python
import functools

import jax
import jax.numpy as jnp
from jax import lax
from jax.experimental import pallas as pl
from jax.experimental.pallas import tpu as pltpu
from jax.sharding import PartitionSpec as P

score_scale = 192.0 ** (-0.5)
route_scale = 2.5
BF, F32 = jnp.bfloat16, jnp.float32
EXTRA = 128
UP, DOWN, SIDE_A, SIDE_B, CORE = range(5)


def chip_grid(n):
    return (4, 2, 2) if n == 32 else (n // 2, 1, 1)


def body(
    n,
    normed_ref, ids_ref, lev_ref, len_ref, place_ref, wg_hbm, wu_hbm, wd_hbm,
    ql_ref, qr_ref, cl_ref, cr_ref,
    moe_ref, att_ref,
    xs, acc, rc, rb, ra, ru, rd, wg, wu, wd, h3, cf, rq, gacc, uacc,
    w_sem, ag_ss, ag_rs, rs_ss, rc_s, rb_s, ra_s, ru_s, rd_s,
):
    Z, Y, X = chip_grid(n)
    plane = Y * X
    planar = plane > 1
    chips = n // 2
    R, D = normed_ref.shape
    F = wg.shape[1]
    top = ids_ref.shape[1]
    me = lax.axis_index("expert")
    c = me % 2
    chip = me // 2
    z = chip // plane
    y = (chip % plane) // X
    x = chip % X
    a = x * (1 - c) + y * c
    b = y * (1 - c) + x * c
    sa = (1 - c) + X * c
    sb = X * (1 - c) + c
    peer_a = me + 2 * (1 - 2 * a) * sa
    peer_b = me + 2 * (1 - 2 * b) * sb
    peer_c = 2 * chip + 1 - c
    up, down = me + 2 * plane, me - 2 * plane

    def at(zz, aa, bb):
        if planar:
            return zz * plane + aa * sa + bb * sb
        return zz

    for src, dst, s in ((wg_hbm, wg, 0), (wu_hbm, wu, 1), (wd_hbm, wd, 2)):
        pltpu.make_async_copy(src.at[0], dst, w_sem.at[s]).start()

    xs[chip, c, :, pl.ds(0, D)] = normed_ref[...]
    lane = lax.broadcasted_iota(jnp.int32, (R, EXTRA), 1)
    tail = jnp.zeros((R, EXTRA), F32)
    for k in range(top):
        tail = jnp.where(lane == k, ids_ref[:, k : k + 1].astype(F32), tail)
        tail = jnp.where(lane == top + k, lev_ref[:, k : k + 1].astype(F32), tail)
    xs[chip, c, :, pl.ds(D, EXTRA)] = tail.astype(BF)

    barrier = pltpu.get_barrier_semaphore()

    def greet(dev):
        pl.semaphore_signal(barrier, inc=1, device_id={"expert": dev})

    greet(peer_c)
    if planar:
        greet(peer_a)
        greet(peer_b)
    pl.when(z < Z - 1)(lambda: greet(up))
    pl.when(z > 0)(lambda: greet(down))
    ends = jnp.where(z == 0, 1, 0) + jnp.where(z == Z - 1, 1, 0)
    pl.semaphore_wait(barrier, (5 if planar else 3) - ends)

    def ag(i, cc, way, dev):
        return pltpu.make_async_remote_copy(
            xs.at[i, cc], xs.at[i, cc], ag_ss.at[way, i], ag_rs.at[i, cc], device_id={"expert": dev}
        )

    def got(i, cc):
        ag(i, cc, CORE, peer_c).wait_recv()

    def share(i):
        if planar:
            ag(i, c, SIDE_A, peer_a).start()
            ag(i, c, SIDE_B, peer_b).start()
        ag(i, c, CORE, peer_c).start()

    pl.when(z < Z - 1)(lambda: ag(chip, c, UP, up).start())
    pl.when(z > 0)(lambda: ag(chip, c, DOWN, down).start())
    share(chip)

    qr = qr_ref[...].astype(F32)
    heads, rope = ql_ref.shape[1], cr_ref.shape[1]
    for h in range(heads):
        rq[h * R : (h + 1) * R, :rope] = qr[:, h * rope : (h + 1) * rope]

    lmax = cl_ref.shape[1]

    def attend(t):
        keys = cl_ref[t]
        rope_q = rq[pl.ds(t, heads, stride=R), :rope].astype(BF)
        s = lax.dot_general(ql_ref[t], keys, (((1,), (1,)), ((), ())), preferred_element_type=F32)
        s = s + jnp.dot(rope_q, cr_ref[t], preferred_element_type=F32)
        s = s * score_scale
        seen = lax.broadcasted_iota(jnp.int32, (heads, lmax), 1) < len_ref[t]
        s = jnp.where(seen, s, -1e30)
        e = jnp.where(seen, jnp.exp(s - jnp.max(s, axis=-1, keepdims=True)), 0.0)
        p = (e / jnp.sum(e, axis=-1, keepdims=True)).astype(BF)
        att_ref[t] = jnp.dot(p, keys, preferred_element_type=F32).astype(BF)

    def from_a(zz):
        i = at(zz, 1 - a, b)
        got(i, c)
        ag(i, c, SIDE_B, peer_b).start()
        ag(i, c, CORE, peer_c).start()

    if planar:
        from_a(z)

    def z_step(d, carry):
        @pl.when(z - d >= 0)
        def _():
            i = at(z - d, a, b)
            got(i, c)
            pl.when(z < Z - 1)(lambda: ag(i, c, UP, up).start())
            share(i)

        @pl.when(z + d < Z)
        def _():
            i = at(z + d, a, b)
            got(i, c)
            pl.when(z > 0)(lambda: ag(i, c, DOWN, down).start())
            share(i)

        if planar:
            pl.when(z - d >= 0)(lambda: from_a(z - d))
            pl.when(z + d < Z)(lambda: from_a(z + d))
        return carry

    lax.fori_loop(1, Z, z_step, 0)

    if planar:
        def from_b(k, carry):
            attend(k)
            i = at(k // 2, k % 2, 1 - b)
            got(i, c)
            ag(i, c, CORE, peer_c).start()
            return carry

        lax.fori_loop(0, 2 * Z, from_b, 0)
        first = min(2 * Z, R)
    else:
        first = 0
    for t in range(first, R):
        attend(t)

    def from_core(i, carry):
        got(i, 1 - c)
        return carry

    lax.fori_loop(0, chips, from_core, 0)

    for src, dst, s in ((wg_hbm, wg, 0), (wu_hbm, wu, 1), (wd_hbm, wd, 2)):
        pltpu.make_async_copy(src.at[0], dst, w_sem.at[s]).wait()
    rows = n * R
    kc = 1024
    gacc[...] = jnp.zeros_like(gacc)
    uacc[...] = jnp.zeros_like(uacc)

    def k_step(k, carry):
        ks = pl.ds(pl.multiple_of(k * kc, kc), kc)
        xk = xs[:, :, :, ks].astype(F32).reshape(rows, kc).astype(BF)
        gacc[...] += jnp.dot(xk, wg[ks, :], preferred_element_type=F32)
        uacc[...] += jnp.dot(xk, wu[ks, :], preferred_element_type=F32)
        return carry

    lax.fori_loop(0, D // kc, k_step, 0)
    g = gacc[...]
    hidden = (g / (1.0 + jnp.exp(-g)) * uacc[...]).astype(BF)
    h3[...] = hidden.astype(F32).reshape(chips, 2, R, F)

    mine = place_ref[me].astype(F32)
    info = xs[:, :, :, pl.ds(D, EXTRA)].astype(F32).reshape(rows, EXTRA)
    levels = [info[:, top + k : top + k + 1] for k in range(top)]
    total = functools.reduce(lambda p, q: p + q, levels)
    coef = jnp.zeros((rows, 1), F32)
    for k in range(top):
        coef = coef + jnp.where(info[:, k : k + 1] == mine, route_scale * levels[k] / total, 0.0)
    cf[...] = jnp.broadcast_to(coef, (rows, EXTRA)).reshape(chips, 2, R, EXTRA)

    nc = 1024

    def down_half(cc):
        hh = h3[:, cc].reshape(chips * R, F).astype(BF)
        scale = cf[:, cc].reshape(chips * R, EXTRA)[:, :1]

        def n_step(k, carry):
            ns = pl.ds(pl.multiple_of(k * nc, nc), nc)
            p = jnp.dot(hh, wd[:, ns], preferred_element_type=F32).astype(BF).astype(F32)
            acc[:, cc, :, ns] = (p * scale).reshape(chips, R, nc).astype(BF)
            return carry

        lax.fori_loop(0, D // nc, n_step, 0)

    def to_core(i):
        return pltpu.make_async_remote_copy(
            acc.at[i, 1 - c], rc.at[i], rs_ss.at[CORE, i], rc_s.at[i], device_id={"expert": peer_c}
        )

    def to_b(zz, aa):
        i = at(zz, aa, 1 - b)
        return pltpu.make_async_remote_copy(
            acc.at[i, c], rb.at[zz, aa], rs_ss.at[SIDE_B, i], rb_s.at[zz, aa], device_id={"expert": peer_b}
        )

    def to_a(zz):
        i = at(zz, 1 - a, b)
        return pltpu.make_async_remote_copy(
            acc.at[i, c], ra.at[zz], rs_ss.at[SIDE_A, i], ra_s.at[zz], device_id={"expert": peer_a}
        )

    def to_up(zz):
        i = at(zz, a, b)
        return pltpu.make_async_remote_copy(
            acc.at[i, c], ru.at[zz], rs_ss.at[UP, i], ru_s.at[zz], device_id={"expert": up}
        )

    def to_down(zz):
        i = at(zz, a, b)
        return pltpu.make_async_remote_copy(
            acc.at[i, c], rd.at[zz], rs_ss.at[DOWN, i], rd_s.at[zz], device_id={"expert": down}
        )

    down_half(1 - c)

    def far(k):
        return jnp.where(z < Z // 2, Z - 1 - k, k)

    def core_send(k, carry):
        if planar:
            q = k % (chips // 2)
            zz, other = far(q // 2), 1 - q % 2
            away = 1 - k // (chips // 2)
            aa = (1 - 2 * a) * away + a
            bb = (1 - 2 * b) * other + b
            to_core(at(zz, aa, bb)).start()
        else:
            to_core(far(k)).start()
        return carry

    lax.fori_loop(0, chips, core_send, 0)
    down_half(c)

    def plus(*terms):
        return functools.reduce(lambda p, q: p + q, [t.astype(F32) for t in terms])

    if planar:
        def b_send(k, carry):
            zz = far(k // 2)
            aa = (1 - 2 * a) * (1 - k % 2) + a
            i = at(zz, aa, 1 - b)
            to_core(i).wait_recv()
            acc[i, c] = plus(acc[i, c], rc[i]).astype(BF)
            to_b(zz, aa).start()
            return carry

        lax.fori_loop(0, 2 * Z, b_send, 0)

        def a_send(k, carry):
            zz = far(k)
            i = at(zz, 1 - a, b)
            to_core(i).wait_recv()
            to_b(zz, 1 - a).wait_recv()
            acc[i, c] = plus(acc[i, c], rc[i], rb[zz, 1 - a]).astype(BF)
            to_a(zz).start()
            return carry

        lax.fori_loop(0, Z, a_send, 0)

    def z_send(k, carry):
        zz = far(k)
        i = at(zz, a, b)
        to_core(i).wait_recv()
        if planar:
            to_b(zz, a).wait_recv()
            to_a(zz).wait_recv()
            total = plus(acc[i, c], rc[i], rb[zz, a], ra[zz])
        else:
            total = plus(acc[i, c], rc[i])

        @pl.when(zz > z)
        def _():
            @pl.when(z > 0)
            def _():
                to_up(zz).wait_recv()
                acc[i, c] = (total + ru[zz].astype(F32)).astype(BF)

            @pl.when(z == 0)
            def _():
                acc[i, c] = total.astype(BF)

            to_up(zz).start()

        @pl.when(zz < z)
        def _():
            @pl.when(z < Z - 1)
            def _():
                to_down(zz).wait_recv()
                acc[i, c] = (total + rd[zz].astype(F32)).astype(BF)

            @pl.when(z == Z - 1)
            def _():
                acc[i, c] = total.astype(BF)

            to_down(zz).start()

        @pl.when(zz == z)
        def _():
            acc[i, c] = total.astype(BF)

        return carry

    lax.fori_loop(0, Z, z_send, 0)

    @pl.when(z == 0)
    def _():
        to_down(z).wait_recv()
        moe_ref[...] = plus(acc[chip, c], rd[z]).astype(BF)

    @pl.when(z == Z - 1)
    def _():
        to_up(z).wait_recv()
        moe_ref[...] = plus(acc[chip, c], ru[z]).astype(BF)

    @pl.when((z > 0) & (z < Z - 1))
    def _():
        to_up(z).wait_recv()
        to_down(z).wait_recv()
        moe_ref[...] = plus(acc[chip, c], ru[z], rd[z]).astype(BF)

    def core_done(i, carry):
        ag(i, c, CORE, peer_c).wait_send()
        to_core(i).wait_send()
        return carry

    lax.fori_loop(0, chips, core_done, 0)

    def z_done(zz, carry):
        i = at(zz, a, b)
        pl.when((zz <= z) & (z < Z - 1))(lambda: ag(i, c, UP, up).wait_send())
        pl.when((zz >= z) & (z > 0))(lambda: ag(i, c, DOWN, down).wait_send())
        pl.when(zz > z)(lambda: to_up(zz).wait_send())
        pl.when(zz < z)(lambda: to_down(zz).wait_send())
        if planar:
            ag(i, c, SIDE_A, peer_a).wait_send()
            to_a(zz).wait_send()
            for aa in range(2):
                ag(at(zz, aa, b), c, SIDE_B, peer_b).wait_send()
                to_b(zz, aa).wait_send()
        return carry

    lax.fori_loop(0, Z, z_done, 0)


def per_device(
    normed, expert_ids, gate_levels, placement, w_gate, w_up, w_down,
    q_latent, q_rope, cache_latent, cache_rope, lengths,
):
    n = lax.axis_size("expert")
    Z, Y, X = chip_grid(n)
    chips = n // 2
    R, D = normed.shape
    F = w_gate.shape[2]
    heads = q_latent.shape[1]
    vmem = pl.BlockSpec(memory_space=pltpu.VMEM)
    smem = pl.BlockSpec(memory_space=pltpu.SMEM)
    hbm = pl.BlockSpec(memory_space=pl.ANY)
    dma = pltpu.SemaphoreType.DMA
    side = Z if Y * X > 1 else 1
    return pl.pallas_call(
        functools.partial(body, n),
        out_shape=(
            jax.ShapeDtypeStruct((R, D), BF),
            jax.ShapeDtypeStruct(q_latent.shape, BF),
        ),
        in_specs=[vmem, vmem, vmem, smem, smem, hbm, hbm, hbm, vmem, vmem, vmem, vmem],
        out_specs=(vmem, vmem),
        scratch_shapes=[
            pltpu.VMEM((chips, 2, R, D + EXTRA), BF),
            pltpu.VMEM((chips, 2, R, D), BF),
            pltpu.VMEM((chips, R, D), BF),
            pltpu.VMEM((side, 2, R, D), BF),
            pltpu.VMEM((side, R, D), BF),
            pltpu.VMEM((Z, R, D), BF),
            pltpu.VMEM((Z, R, D), BF),
            pltpu.VMEM((D, F), BF),
            pltpu.VMEM((D, F), BF),
            pltpu.VMEM((F, D), BF),
            pltpu.VMEM((chips, 2, R, F), F32),
            pltpu.VMEM((chips, 2, R, EXTRA), F32),
            pltpu.VMEM((heads * R, 128), F32),
            pltpu.VMEM((n * R, F), F32),
            pltpu.VMEM((n * R, F), F32),
            dma((3,)),
            dma((5, chips)),
            dma((chips, 2)),
            dma((5, chips)),
            dma((chips,)),
            dma((side, 2)),
            dma((side,)),
            dma((Z,)),
            dma((Z,)),
        ],
        compiler_params=pltpu.CompilerParams(
            collective_id=0, has_side_effects=True, vmem_limit_bytes=60 << 20
        ),
        cost_estimate=pl.CostEstimate(flops=3 * 10**9, bytes_accessed=13 * 10**6, transcendentals=300000),
    )(
        normed, expert_ids, gate_levels, lengths, placement, w_gate, w_up, w_down,
        q_latent, q_rope, cache_latent, cache_rope,
    )


def solution(mesh):
    rows = ("groups", "expert")
    in_specs = (
        P(rows, None), P(rows, None), P(rows, None), P(),
        P("expert", None, None), P("expert", None, None), P("expert", None, None),
        P(rows, None, None), P(rows, None), P(rows, None, None), P(rows, None, None), P(rows),
    )
    out_specs = (P(rows, None), P(rows, None, None))
    return jax.shard_map(
        per_device, mesh=mesh, in_specs=in_specs, out_specs=out_specs, check_vma=False
    )
```

time: 204 us -> 76.5 us (0.38)
  blocking collectives: 90.2 us -> 0 us
  waiting for transfers between devices: 80.3 us -> 0 us
  Pallas kernels: 0 us -> 69.2 us
  matrix products: 17.9 us -> 0 us
  starting transfers between devices: 3.69 us -> 0 us
  local copies, waits for them, and re-layouts: 9.32 us -> 6.11 us
    all_to_all x1 -> x0, blocking collectives: 90.2 us -> none  [per_device(): lax.all_to_all(outgoing, 'expert', split_axis=0, concat_axis=0, tiled=True)]
    all_to_all x1 -> x0, waiting for transfers between devices: 80.3 us -> none  [per_device(): lax.all_to_all(partials, 'expert', split_axis=0, concat_axis=0, tiled=True)]
    pallas_call x0 -> x1, Pallas kernels: none -> 69.2 us  [per_device(): pl.pallas_call(functools.partial(body, n), out_shape=(jax.ShapeDtypeStruc...]
    dot_general x7 -> x0, matrix products: 17.9 us -> none  [the longest x1 7.15 us: expert_block(): jnp.dot(hidden, down_mat, preferred_element_type=jnp.float32)]
    reshape x3 -> x0, local copies, waits for them, and re-layouts: 7.98 us -> none  [the longest x1 4.55 us: expert_block(): return partial_value.reshape(shape[0], shape[1], down_mat.shape[1])]
    unnamed x16 -> x4, local copies, waits for them, and re-layouts: 0.04 us -> 6.11 us
    all_to_all x1 -> x0, starting transfers between devices: 3.69 us -> none  [per_device(): lax.all_to_all(partials, 'expert', split_axis=0, concat_axis=0, tiled=True)]
  transfers between devices with their start and end apart: 1 -> 0, of which waited for: 1 -> 0; matrix products, arithmetic and copies ran while one was open for 1% -> 0% of each run, Pallas kernels for 0% -> 0%
where the time goes in v1:
time: 76.5 us; the launch traced here: 75.9 us
  Pallas kernels  69.2 us (90%)
  local copies, waits for them, and re-layouts  6.11 us (8%)
    pallas_call x1, Pallas kernels, per_device(): pl.pallas_call(functools.partial(body, n), out_shape=(jax.ShapeDtypeStruc...  69.2 us
    unnamed x4, local copies, waits for them, and re-layouts  6.11 us

profile of v1, /device:TPU:0, one launch (start us, length us, event | category | flops | bytes accessed | tf_op | source)
XLA Modules:
  0.0 75.9 jit_solution(860130857141881609)
XLA Ops:
  0.6 1.3 %copy.14.ids_ref = s32[8,2]{1,0:T(8,128)} copy(s32[8,2]{0,1:T(2,128)} %param.13) | data formatting | bytes 128 | tf_op args[1]
  2.0 1.3 %copy.15.lev_ref = s32[8,2]{1,0:T(8,128)} copy(s32[8,2]{0,1:T(2,128)} %param.14) | data formatting | bytes 128 | tf_op args[2]
  3.3 69.2 %shard_map.131 = (bf16[8,7168]{1,0:T(8,128)(2,1)}, bf16[8,64,512]{2,1,0:T(8,128)(2,1)}) custom-call(bf16[8,7168]{1,0:T(8,128)(2,1)} %normed_ref.1, s32[8,2]{1,0:T(8,128)} %copy.14.ids_ref, s32[8,2]{1,0:T(8,128)} %copy.15.lev_ref, s32[8]{0:T(128)} %len_ref.1, s32[32]{0:T(128)} %place_ref.1, bf16[1,7168,256]{2,1,0:T(8,128)(2,1)} %wg_hbm.1, ...), custom_call_target="tpu_custom_call" | custom-call | flops 3000000000 | bytes 13000000 | tf_op jit(solution)/shard_map/pallas_call | solution.py:387
  72.5 1.6 %copy.18 = bf16[8,7168]{1,0:T(8,128)(2,1)} copy(bf16[8,7168]{1,0:T(8,128)(2,1)} %get-tuple-element.4) | data formatting | bytes 229376
  74.1 1.9 %copy.19 = bf16[8,64,512]{2,1,0:T(8,128)(2,1)} copy(bf16[8,64,512]{2,1,0:T(8,128)(2,1)} %get-tuple-element.5) | data formatting | bytes 1048576

commit v2 on v1

--- a/solution.py
+++ b/solution.py
@@ -11,7 +11,7 @@
 route_scale = 2.5
 BF, F32 = jnp.bfloat16, jnp.float32
 EXTRA = 128
-UP, DOWN, SIDE_A, SIDE_B, CORE = range(5)
+SIDE_A, SIDE_B, CORE = range(3)
 
 
 def chip_grid(n):
@@ -23,8 +23,8 @@
     normed_ref, ids_ref, lev_ref, len_ref, place_ref, wg_hbm, wu_hbm, wd_hbm,
     ql_ref, qr_ref, cl_ref, cr_ref,
     moe_ref, att_ref,
-    xs, acc, rc, rb, ra, ru, rd, wg, wu, wd, h3, cf, rq, gacc, uacc,
-    w_sem, ag_ss, ag_rs, rs_ss, rc_s, rb_s, ra_s, ru_s, rd_s,
+    xs, acc, rc, rb, ra, rz, wg, wu, wd, h3, cf, rq, gacc, uacc,
+    w_sem, ag_ss, ag_rs, agz_ss, rs_ss, rsz_ss, rc_s, rb_s, ra_s, rz_s,
 ):
     Z, Y, X = chip_grid(n)
     plane = Y * X
@@ -32,7 +32,7 @@
     chips = n // 2
     R, D = normed_ref.shape
     F = wg.shape[1]
-    top = ids_ref.shape[1]
+    top = ids_ref.shape[0]
     me = lax.axis_index("expert")
     c = me % 2
     chip = me // 2
@@ -46,7 +46,6 @@
     peer_a = me + 2 * (1 - 2 * a) * sa
     peer_b = me + 2 * (1 - 2 * b) * sb
     peer_c = 2 * chip + 1 - c
-    up, down = me + 2 * plane, me - 2 * plane
 
     def at(zz, aa, bb):
         if planar:
@@ -58,10 +57,16 @@
 
     xs[chip, c, :, pl.ds(0, D)] = normed_ref[...]
     lane = lax.broadcasted_iota(jnp.int32, (R, EXTRA), 1)
+    same = lax.broadcasted_iota(jnp.int32, (R, R), 0) == lax.broadcasted_iota(jnp.int32, (R, R), 1)
+
+    def column(ref, k):
+        row = jnp.broadcast_to(ref[k : k + 1, :].astype(F32), (R, R))
+        return jnp.sum(jnp.where(same, row, 0.0), axis=1, keepdims=True)
+
     tail = jnp.zeros((R, EXTRA), F32)
     for k in range(top):
-        tail = jnp.where(lane == k, ids_ref[:, k : k + 1].astype(F32), tail)
-        tail = jnp.where(lane == top + k, lev_ref[:, k : k + 1].astype(F32), tail)
+        tail = jnp.where(lane == k, column(ids_ref, k), tail)
+        tail = jnp.where(lane == top + k, column(lev_ref, k), tail)
     xs[chip, c, :, pl.ds(D, EXTRA)] = tail.astype(BF)
 
     barrier = pltpu.get_barrier_semaphore()
@@ -73,10 +78,9 @@
     if planar:
         greet(peer_a)
         greet(peer_b)
-    pl.when(z < Z - 1)(lambda: greet(up))
-    pl.when(z > 0)(lambda: greet(down))
-    ends = jnp.where(z == 0, 1, 0) + jnp.where(z == Z - 1, 1, 0)
-    pl.semaphore_wait(barrier, (5 if planar else 3) - ends)
+    for d in range(1, Z):
+        greet(me + 2 * plane * ((z + d) % Z - z))
+    pl.semaphore_wait(barrier, Z - 1 + (3 if planar else 1))
 
     def ag(i, cc, way, dev):
         return pltpu.make_async_remote_copy(
@@ -92,9 +96,23 @@
             ag(i, c, SIDE_B, peer_b).start()
         ag(i, c, CORE, peer_c).start()
 
-    pl.when(z < Z - 1)(lambda: ag(chip, c, UP, up).start())
-    pl.when(z > 0)(lambda: ag(chip, c, DOWN, down).start())
+    def column_dev(zz):
+        return me + 2 * plane * (zz - z)
+
+    def ag_z(zz):
+        return pltpu.make_async_remote_copy(
+            xs.at[chip, c], xs.at[chip, c], agz_ss.at[zz], ag_rs.at[chip, c],
+            device_id={"expert": column_dev(zz)},
+        )
+
     share(chip)
+
+    def z_out(d, carry):
+        pl.when(z - d >= 0)(lambda: ag_z(z - d).start())
+        pl.when(z + d < Z)(lambda: ag_z(z + d).start())
+        return carry
+
+    lax.fori_loop(1, Z, z_out, 0)
 
     qr = qr_ref[...].astype(F32)
     heads, rope = ql_ref.shape[1], cr_ref.shape[1]
@@ -129,14 +147,12 @@
         def _():
             i = at(z - d, a, b)
             got(i, c)
-            pl.when(z < Z - 1)(lambda: ag(i, c, UP, up).start())
             share(i)
 
         @pl.when(z + d < Z)
         def _():
             i = at(z + d, a, b)
             got(i, c)
-            pl.when(z > 0)(lambda: ag(i, c, DOWN, down).start())
             share(i)
 
         if planar:
@@ -149,7 +165,7 @@
     if planar:
         def from_b(k, carry):
             attend(k)
-            i = at(k // 2, k % 2, 1 - b)
+            i = at((z + k // 2) % Z, k % 2, 1 - b)
             got(i, c)
             ag(i, c, CORE, peer_c).start()
             return carry
@@ -226,22 +242,22 @@
             acc.at[i, c], ra.at[zz], rs_ss.at[SIDE_A, i], ra_s.at[zz], device_id={"expert": peer_a}
         )
 
-    def to_up(zz):
-        i = at(zz, a, b)
-        return pltpu.make_async_remote_copy(
-            acc.at[i, c], ru.at[zz], rs_ss.at[UP, i], ru_s.at[zz], device_id={"expert": up}
-        )
-
-    def to_down(zz):
-        i = at(zz, a, b)
-        return pltpu.make_async_remote_copy(
-            acc.at[i, c], rd.at[zz], rs_ss.at[DOWN, i], rd_s.at[zz], device_id={"expert": down}
+    def to_z(zz):
+        return pltpu.make_async_remote_copy(
+            acc.at[at(zz, a, b), c], rz.at[z], rsz_ss.at[zz], rz_s.at[z],
+            device_id={"expert": column_dev(zz)},
+        )
+
+    def from_z(zz):
+        return pltpu.make_async_remote_copy(
+            acc.at[chip, c], rz.at[zz], rsz_ss.at[zz], rz_s.at[zz],
+            device_id={"expert": column_dev(zz)},
         )
 
     down_half(1 - c)
 
     def far(k):
-        return jnp.where(z < Z // 2, Z - 1 - k, k)
+        return (z + 1 + k) % Z
 
     def core_send(k, carry):
         if planar:
@@ -273,77 +289,40 @@
 
         lax.fori_loop(0, 2 * Z, b_send, 0)
 
-        def a_send(k, carry):
+        def a_send(k):
             zz = far(k)
             i = at(zz, 1 - a, b)
             to_core(i).wait_recv()
             to_b(zz, 1 - a).wait_recv()
             acc[i, c] = plus(acc[i, c], rc[i], rb[zz, 1 - a]).astype(BF)
             to_a(zz).start()
-            return carry
-
-        lax.fori_loop(0, Z, a_send, 0)
-
-    def z_send(k, carry):
-        zz = far(k)
+
+        a_send(0)
+
+    def column_sum(zz):
         i = at(zz, a, b)
         to_core(i).wait_recv()
         if planar:
             to_b(zz, a).wait_recv()
             to_a(zz).wait_recv()
-            total = plus(acc[i, c], rc[i], rb[zz, a], ra[zz])
-        else:
-            total = plus(acc[i, c], rc[i])
-
-        @pl.when(zz > z)
-        def _():
-            @pl.when(z > 0)
-            def _():
-                to_up(zz).wait_recv()
-                acc[i, c] = (total + ru[zz].astype(F32)).astype(BF)
-
-            @pl.when(z == 0)
-            def _():
-                acc[i, c] = total.astype(BF)
-
-            to_up(zz).start()
-
-        @pl.when(zz < z)
-        def _():
-            @pl.when(z < Z - 1)
-            def _():
-                to_down(zz).wait_recv()
-                acc[i, c] = (total + rd[zz].astype(F32)).astype(BF)
-
-            @pl.when(z == Z - 1)
-            def _():
-                acc[i, c] = total.astype(BF)
-
-            to_down(zz).start()
-
-        @pl.when(zz == z)
-        def _():
-            acc[i, c] = total.astype(BF)
-
-        return carry
-
-    lax.fori_loop(0, Z, z_send, 0)
-
-    @pl.when(z == 0)
-    def _():
-        to_down(z).wait_recv()
-        moe_ref[...] = plus(acc[chip, c], rd[z]).astype(BF)
-
-    @pl.when(z == Z - 1)
-    def _():
-        to_up(z).wait_recv()
-        moe_ref[...] = plus(acc[chip, c], ru[z]).astype(BF)
-
-    @pl.when((z > 0) & (z < Z - 1))
-    def _():
-        to_up(z).wait_recv()
-        to_down(z).wait_recv()
-        moe_ref[...] = plus(acc[chip, c], ru[z], rd[z]).astype(BF)
+            return plus(acc[i, c], rc[i], rb[zz, a], ra[zz])
+        return plus(acc[i, c], rc[i])
+
+    def z_send(k, carry):
+        if planar:
+            a_send(k + 1)
+        zz = far(k)
+        acc[at(zz, a, b), c] = column_sum(zz).astype(BF)
+        to_z(zz).start()
+        return carry
+
+    lax.fori_loop(0, Z - 1, z_send, 0)
+    result = column_sum(z)
+    for d in range(1, Z):
+        zz = (z + d) % Z
+        from_z(zz).wait_recv()
+        result = result + rz[zz].astype(F32)
+    moe_ref[...] = result.astype(BF)
 
     def core_done(i, carry):
         ag(i, c, CORE, peer_c).wait_send()
@@ -354,10 +333,12 @@
 
     def z_done(zz, carry):
         i = at(zz, a, b)
-        pl.when((zz <= z) & (z < Z - 1))(lambda: ag(i, c, UP, up).wait_send())
-        pl.when((zz >= z) & (z > 0))(lambda: ag(i, c, DOWN, down).wait_send())
-        pl.when(zz > z)(lambda: to_up(zz).wait_send())
-        pl.when(zz < z)(lambda: to_down(zz).wait_send())
+
+        @pl.when(zz != z)
+        def _():
+            ag_z(zz).wait_send()
+            to_z(zz).wait_send()
+
         if planar:
             ag(i, c, SIDE_A, peer_a).wait_send()
             to_a(zz).wait_send()
@@ -399,7 +380,6 @@
             pltpu.VMEM((side, 2, R, D), BF),
             pltpu.VMEM((side, R, D), BF),
             pltpu.VMEM((Z, R, D), BF),
-            pltpu.VMEM((Z, R, D), BF),
             pltpu.VMEM((D, F), BF),
             pltpu.VMEM((D, F), BF),
             pltpu.VMEM((F, D), BF),
@@ -409,13 +389,14 @@
             pltpu.VMEM((n * R, F), F32),
             pltpu.VMEM((n * R, F), F32),
             dma((3,)),
-            dma((5, chips)),
+            dma((3, chips)),
             dma((chips, 2)),
-            dma((5, chips)),
+            dma((Z,)),
+            dma((3, chips)),
+            dma((Z,)),
             dma((chips,)),
             dma((side, 2)),
             dma((side,)),
-            dma((Z,)),
             dma((Z,)),
         ],
         compiler_params=pltpu.CompilerParams(
@@ -423,7 +404,7 @@
         ),
         cost_estimate=pl.CostEstimate(flops=3 * 10**9, bytes_accessed=13 * 10**6, transcendentals=300000),
     )(
-        normed, expert_ids, gate_levels, lengths, placement, w_gate, w_up, w_down,
+        normed, expert_ids.T, gate_levels.T, lengths, placement, w_gate, w_up, w_down,
         q_latent, q_rope, cache_latent, cache_rope,
     )
 

time: 76.5 us -> 67.8 us (0.89)
  Pallas kernels: 69.2 us -> 63.5 us
  local copies, waits for them, and re-layouts: 6.11 us -> 3.42 us
    pallas_call x1, Pallas kernels: 69.2 us -> 63.5 us  [per_device(): pl.pallas_call(functools.partial(body, n), out_shape=(jax.ShapeDtypeStruc...]
    unnamed x4 -> x2, local copies, waits for them, and re-layouts: 6.11 us -> 3.42 us
where the time goes in v2:
time: 67.8 us; the launch traced here: 67.6 us
  Pallas kernels  63.5 us (94%)
  local copies, waits for them, and re-layouts  3.42 us (5%)
    pallas_call x1, Pallas kernels, per_device(): pl.pallas_call(functools.partial(body, n), out_shape=(jax.ShapeDtypeStruc...  63.5 us
    unnamed x2, local copies, waits for them, and re-layouts  3.42 us

profile of v2, /device:TPU:0, one launch (start us, length us, event | category | flops | bytes accessed | tf_op | source)
XLA Modules:
  0.0 67.6 jit_solution(3864346189858170558)
XLA Ops:
  0.6 63.5 %shard_map.131 = (bf16[8,7168]{1,0:T(8,128)(2,1)}, bf16[8,64,512]{2,1,0:T(8,128)(2,1)}) custom-call(bf16[8,7168]{1,0:T(8,128)(2,1)} %normed_ref.1, s32[2,8]{1,0:T(2,128)} %bitcast.2, s32[2,8]{1,0:T(2,128)} %bitcast.3, s32[8]{0:T(128)} %len_ref.1, s32[32]{0:T(128)} %place_ref.1, bf16[1,7168,256]{2,1,0:T(8,128)(2,1)} %wg_hbm.1, bf16[1,7168,256]{2,1,0:T(8,128)(2,1)} %wu_hbm.1, ...), custom_call_target="tpu_custom_call" | custom-call | flops 3000000000 | bytes 13000000 | tf_op jit(solution)/shard_map/pallas_call | solution.py:368
  64.2 1.6 %copy.16 = bf16[8,7168]{1,0:T(8,128)(2,1)} copy(bf16[8,7168]{1,0:T(8,128)(2,1)} %get-tuple-element.4) | data formatting | bytes 229376
  65.7 1.9 %copy.17 = bf16[8,64,512]{2,1,0:T(8,128)(2,1)} copy(bf16[8,64,512]{2,1,0:T(8,128)(2,1)} %get-tuple-element.5) | data formatting | bytes 1048576

commit v3 on v2

--- a/solution.py
+++ b/solution.py
@@ -11,20 +11,25 @@
 route_scale = 2.5
 BF, F32 = jnp.bfloat16, jnp.float32
 EXTRA = 128
-SIDE_A, SIDE_B, CORE = range(3)
+PA, PR = 3, 2
+SIDE_A, SIDE_B = range(2)
 
 
 def chip_grid(n):
     return (4, 2, 2) if n == 32 else (n // 2, 1, 1)
+
+
+def parts(cols, most):
+    return max(p for p in range(1, most + 1) if cols % (128 * p) == 0)
 
 
 def body(
     n,
     normed_ref, ids_ref, lev_ref, len_ref, place_ref, wg_hbm, wu_hbm, wd_hbm,
-    ql_ref, qr_ref, cl_ref, cr_ref,
-    moe_ref, att_ref,
-    xs, acc, rc, rb, ra, rz, wg, wu, wd, h3, cf, rq, gacc, uacc,
-    w_sem, ag_ss, ag_rs, agz_ss, rs_ss, rsz_ss, rc_s, rb_s, ra_s, rz_s,
+    ql_hbm, qr_ref, cl_hbm, cr_hbm,
+    moe_ref, att_hbm,
+    xs, acc, rc, rb, ra, rz, wg, wu, wd, h3, cf, rq, gacc, uacc, ql_ref, cl_ref, cr_ref, att_ref,
+    w_sem, in_sem, out_sem, ag_ss, ag_rs, agz_ss, agc_ss, agc_rs, rs_ss, rsz_ss, rsc_ss, rc_s, rb_s, ra_s, rz_s,
 ):
     Z, Y, X = chip_grid(n)
     plane = Y * X
@@ -52,23 +57,6 @@
             return zz * plane + aa * sa + bb * sb
         return zz
 
-    for src, dst, s in ((wg_hbm, wg, 0), (wu_hbm, wu, 1), (wd_hbm, wd, 2)):
-        pltpu.make_async_copy(src.at[0], dst, w_sem.at[s]).start()
-
-    xs[chip, c, :, pl.ds(0, D)] = normed_ref[...]
-    lane = lax.broadcasted_iota(jnp.int32, (R, EXTRA), 1)
-    same = lax.broadcasted_iota(jnp.int32, (R, R), 0) == lax.broadcasted_iota(jnp.int32, (R, R), 1)
-
-    def column(ref, k):
-        row = jnp.broadcast_to(ref[k : k + 1, :].astype(F32), (R, R))
-        return jnp.sum(jnp.where(same, row, 0.0), axis=1, keepdims=True)
-
-    tail = jnp.zeros((R, EXTRA), F32)
-    for k in range(top):
-        tail = jnp.where(lane == k, column(ids_ref, k), tail)
-        tail = jnp.where(lane == top + k, column(lev_ref, k), tail)
-    xs[chip, c, :, pl.ds(D, EXTRA)] = tail.astype(BF)
-
     barrier = pltpu.get_barrier_semaphore()
 
     def greet(dev):
@@ -80,39 +68,74 @@
         greet(peer_b)
     for d in range(1, Z):
         greet(me + 2 * plane * ((z + d) % Z - z))
+    for src, dst, s in ((wg_hbm, wg, 0), (wu_hbm, wu, 1), (wd_hbm, wd, 2)):
+        pltpu.make_async_copy(src.at[0], dst, w_sem.at[s]).start()
+
+    for k, (src, dst) in enumerate(((ql_hbm, ql_ref), (cl_hbm, cl_ref), (cr_hbm, cr_ref))):
+        pltpu.make_async_copy(src, dst, in_sem.at[k]).start()
+
+    xs[chip, c, :, pl.ds(0, D)] = normed_ref[...]
+    lane = lax.broadcasted_iota(jnp.int32, (R, EXTRA), 1)
+    same = lax.broadcasted_iota(jnp.int32, (R, R), 0) == lax.broadcasted_iota(jnp.int32, (R, R), 1)
+
+    def column(ref, k):
+        row = jnp.broadcast_to(ref[k : k + 1, :].astype(F32), (R, R))
+        return jnp.sum(jnp.where(same, row, 0.0), axis=1, keepdims=True)
+
+    tail = jnp.zeros((R, EXTRA), F32)
+    for k in range(top):
+        tail = jnp.where(lane == k, column(ids_ref, k), tail)
+        tail = jnp.where(lane == top + k, column(lev_ref, k), tail)
+    xs[chip, c, :, pl.ds(D, EXTRA)] = tail.astype(BF)
+
     pl.semaphore_wait(barrier, Z - 1 + (3 if planar else 1))
 
-    def ag(i, cc, way, dev):
-        return pltpu.make_async_remote_copy(
-            xs.at[i, cc], xs.at[i, cc], ag_ss.at[way, i], ag_rs.at[i, cc], device_id={"expert": dev}
-        )
-
-    def got(i, cc):
-        ag(i, cc, CORE, peer_c).wait_recv()
-
-    def share(i):
-        if planar:
-            ag(i, c, SIDE_A, peer_a).start()
-            ag(i, c, SIDE_B, peer_b).start()
-        ag(i, c, CORE, peer_c).start()
+    pa = ag_rs.shape[1]
+    wa = (D + EXTRA) // pa
+
+    def ag(i, p, way, dev):
+        part = xs.at[i, c, :, pl.ds(p * wa, wa)]
+        return pltpu.make_async_remote_copy(
+            part, part, ag_ss.at[way, i, p], ag_rs.at[i, p], device_id={"expert": dev}
+        )
+
+    def ag_core(i, cc):
+        return pltpu.make_async_remote_copy(
+            xs.at[i, cc], xs.at[i, cc], agc_ss.at[i], agc_rs.at[i], device_id={"expert": peer_c}
+        )
+
+    def got(i, p):
+        ag(i, p, SIDE_A, peer_a).wait_recv()
+
+    def ag_z(zz, p, way, dev):
+        i = at(zz, a, b)
+        part = xs.at[i, c, :, pl.ds(p * wa, wa)]
+        return pltpu.make_async_remote_copy(
+            part, part, agz_ss.at[way, zz, p], ag_rs.at[i, p], device_id={"expert": dev}
+        )
+
+    def go_up(zz, p):
+        pl.when(z < Z - 1)(lambda: ag_z(zz, p, 0, me + 2 * plane).start())
+
+    def go_down(zz, p):
+        pl.when(z > 0)(lambda: ag_z(zz, p, 1, me - 2 * plane).start())
+
+    def share(zz, wait, *onward):
+        i = at(zz, a, b)
+        for p in range(pa):
+            if wait:
+                got(i, p)
+            for step in onward:
+                step(zz, p)
+            if planar:
+                ag(i, p, SIDE_A, peer_a).start()
+                ag(i, p, SIDE_B, peer_b).start()
+        ag_core(i, c).start()
 
     def column_dev(zz):
         return me + 2 * plane * (zz - z)
 
-    def ag_z(zz):
-        return pltpu.make_async_remote_copy(
-            xs.at[chip, c], xs.at[chip, c], agz_ss.at[zz], ag_rs.at[chip, c],
-            device_id={"expert": column_dev(zz)},
-        )
-
-    share(chip)
-
-    def z_out(d, carry):
-        pl.when(z - d >= 0)(lambda: ag_z(z - d).start())
-        pl.when(z + d < Z)(lambda: ag_z(z + d).start())
-        return carry
-
-    lax.fori_loop(1, Z, z_out, 0)
+    share(z, False, go_up, go_down)
 
     qr = qr_ref[...].astype(F32)
     heads, rope = ql_ref.shape[1], cr_ref.shape[1]
@@ -120,6 +143,8 @@
         rq[h * R : (h + 1) * R, :rope] = qr[:, h * rope : (h + 1) * rope]
 
     lmax = cl_ref.shape[1]
+    for k, (src, dst) in enumerate(((ql_hbm, ql_ref), (cl_hbm, cl_ref), (cr_hbm, cr_ref))):
+        pltpu.make_async_copy(src, dst, in_sem.at[k]).wait()
 
     def attend(t):
         keys = cl_ref[t]
@@ -135,26 +160,17 @@
 
     def from_a(zz):
         i = at(zz, 1 - a, b)
-        got(i, c)
-        ag(i, c, SIDE_B, peer_b).start()
-        ag(i, c, CORE, peer_c).start()
+        for p in range(pa):
+            got(i, p)
+            ag(i, p, SIDE_B, peer_b).start()
+        ag_core(i, c).start()
 
     if planar:
         from_a(z)
 
     def z_step(d, carry):
-        @pl.when(z - d >= 0)
-        def _():
-            i = at(z - d, a, b)
-            got(i, c)
-            share(i)
-
-        @pl.when(z + d < Z)
-        def _():
-            i = at(z + d, a, b)
-            got(i, c)
-            share(i)
-
+        pl.when(z - d >= 0)(lambda: share(z - d, True, go_up))
+        pl.when(z + d < Z)(lambda: share(z + d, True, go_down))
         if planar:
             pl.when(z - d >= 0)(lambda: from_a(z - d))
             pl.when(z + d < Z)(lambda: from_a(z + d))
@@ -166,8 +182,9 @@
         def from_b(k, carry):
             attend(k)
             i = at((z + k // 2) % Z, k % 2, 1 - b)
-            got(i, c)
-            ag(i, c, CORE, peer_c).start()
+            for p in range(pa):
+                got(i, p)
+            ag_core(i, c).start()
             return carry
 
         lax.fori_loop(0, 2 * Z, from_b, 0)
@@ -177,8 +194,10 @@
     for t in range(first, R):
         attend(t)
 
+    pltpu.make_async_copy(att_ref, att_hbm, out_sem).start()
+
     def from_core(i, carry):
-        got(i, 1 - c)
+        ag_core(i, 1 - c).wait_recv()
         return carry
 
     lax.fori_loop(0, chips, from_core, 0)
@@ -225,33 +244,41 @@
 
         lax.fori_loop(0, D // nc, n_step, 0)
 
+    pr = rz_s.shape[1]
+    wr = D // pr
+
+    def cols(p):
+        return pl.ds(p * wr, wr)
+
     def to_core(i):
         return pltpu.make_async_remote_copy(
-            acc.at[i, 1 - c], rc.at[i], rs_ss.at[CORE, i], rc_s.at[i], device_id={"expert": peer_c}
-        )
-
-    def to_b(zz, aa):
+            acc.at[i, 1 - c], rc.at[i], rsc_ss.at[i], rc_s.at[i], device_id={"expert": peer_c}
+        )
+
+    def to_b(zz, aa, p):
         i = at(zz, aa, 1 - b)
         return pltpu.make_async_remote_copy(
-            acc.at[i, c], rb.at[zz, aa], rs_ss.at[SIDE_B, i], rb_s.at[zz, aa], device_id={"expert": peer_b}
-        )
-
-    def to_a(zz):
+            acc.at[i, c, :, cols(p)], rb.at[zz, aa, :, cols(p)], rs_ss.at[SIDE_B, i, p],
+            rb_s.at[zz, aa, p], device_id={"expert": peer_b},
+        )
+
+    def to_a(zz, p):
         i = at(zz, 1 - a, b)
         return pltpu.make_async_remote_copy(
-            acc.at[i, c], ra.at[zz], rs_ss.at[SIDE_A, i], ra_s.at[zz], device_id={"expert": peer_a}
-        )
-
-    def to_z(zz):
-        return pltpu.make_async_remote_copy(
-            acc.at[at(zz, a, b), c], rz.at[z], rsz_ss.at[zz], rz_s.at[z],
-            device_id={"expert": column_dev(zz)},
-        )
-
-    def from_z(zz):
-        return pltpu.make_async_remote_copy(
-            acc.at[chip, c], rz.at[zz], rsz_ss.at[zz], rz_s.at[zz],
-            device_id={"expert": column_dev(zz)},
+            acc.at[i, c, :, cols(p)], ra.at[zz, :, cols(p)], rs_ss.at[SIDE_A, i, p],
+            ra_s.at[zz, p], device_id={"expert": peer_a},
+        )
+
+    def to_z(zz, p):
+        return pltpu.make_async_remote_copy(
+            acc.at[at(zz, a, b), c, :, cols(p)], rz.at[z, :, cols(p)], rsz_ss.at[zz, p],
+            rz_s.at[z, p], device_id={"expert": column_dev(zz)},
+        )
+
+    def from_z(zz, p):
+        return pltpu.make_async_remote_copy(
+            acc.at[chip, c, :, cols(p)], rz.at[zz, :, cols(p)], rsz_ss.at[zz, p],
+            rz_s.at[zz, p], device_id={"expert": column_dev(zz)},
         )
 
     down_half(1 - c)
@@ -284,7 +311,8 @@
             i = at(zz, aa, 1 - b)
             to_core(i).wait_recv()
             acc[i, c] = plus(acc[i, c], rc[i]).astype(BF)
-            to_b(zz, aa).start()
+            for p in range(pr):
+                to_b(zz, aa, p).start()
             return carry
 
         lax.fori_loop(0, 2 * Z, b_send, 0)
@@ -293,39 +321,47 @@
             zz = far(k)
             i = at(zz, 1 - a, b)
             to_core(i).wait_recv()
-            to_b(zz, 1 - a).wait_recv()
-            acc[i, c] = plus(acc[i, c], rc[i], rb[zz, 1 - a]).astype(BF)
-            to_a(zz).start()
+            for p in range(pr):
+                to_b(zz, 1 - a, p).wait_recv()
+                cp = cols(p)
+                acc[i, c, :, cp] = plus(acc[i, c, :, cp], rc[i, :, cp], rb[zz, 1 - a, :, cp]).astype(BF)
+                to_a(zz, p).start()
 
         a_send(0)
 
-    def column_sum(zz):
+    def column_sum(zz, p):
         i = at(zz, a, b)
-        to_core(i).wait_recv()
-        if planar:
-            to_b(zz, a).wait_recv()
-            to_a(zz).wait_recv()
-            return plus(acc[i, c], rc[i], rb[zz, a], ra[zz])
-        return plus(acc[i, c], rc[i])
+        cp = cols(p)
+        if planar:
+            to_b(zz, a, p).wait_recv()
+            to_a(zz, p).wait_recv()
+            return plus(acc[i, c, :, cp], rc[i, :, cp], rb[zz, a, :, cp], ra[zz, :, cp])
+        return plus(acc[i, c, :, cp], rc[i, :, cp])
 
     def z_send(k, carry):
         if planar:
             a_send(k + 1)
         zz = far(k)
-        acc[at(zz, a, b), c] = column_sum(zz).astype(BF)
-        to_z(zz).start()
+        to_core(at(zz, a, b)).wait_recv()
+        for p in range(pr):
+            acc[at(zz, a, b), c, :, cols(p)] = column_sum(zz, p).astype(BF)
+            to_z(zz, p).start()
         return carry
 
     lax.fori_loop(0, Z - 1, z_send, 0)
-    result = column_sum(z)
-    for d in range(1, Z):
-        zz = (z + d) % Z
-        from_z(zz).wait_recv()
-        result = result + rz[zz].astype(F32)
-    moe_ref[...] = result.astype(BF)
+    to_core(chip).wait_recv()
+    for p in range(pr):
+        result = column_sum(z, p)
+        for d in range(1, Z):
+            zz = (z + d) % Z
+            from_z(zz, p).wait_recv()
+            result = result + rz[zz, :, cols(p)].astype(F32)
+        moe_ref[:, cols(p)] = result.astype(BF)
+
+    pltpu.make_async_copy(att_ref, att_hbm, out_sem).wait()
 
     def core_done(i, carry):
-        ag(i, c, CORE, peer_c).wait_send()
+        ag_core(i, c).wait_send()
         to_core(i).wait_send()
         return carry
 
@@ -336,15 +372,21 @@
 
         @pl.when(zz != z)
         def _():
-            ag_z(zz).wait_send()
-            to_z(zz).wait_send()
-
-        if planar:
-            ag(i, c, SIDE_A, peer_a).wait_send()
-            to_a(zz).wait_send()
-            for aa in range(2):
-                ag(at(zz, aa, b), c, SIDE_B, peer_b).wait_send()
-                to_b(zz, aa).wait_send()
+            for p in range(pr):
+                to_z(zz, p).wait_send()
+
+        for p in range(pa):
+            pl.when((zz <= z) & (z < Z - 1))(lambda: ag_z(zz, p, 0, me + 2 * plane).wait_send())
+            pl.when((zz >= z) & (z > 0))(lambda: ag_z(zz, p, 1, me - 2 * plane).wait_send())
+        if planar:
+            for p in range(pa):
+                ag(i, p, SIDE_A, peer_a).wait_send()
+                for aa in range(2):
+                    ag(at(zz, aa, b), p, SIDE_B, peer_b).wait_send()
+            for p in range(pr):
+                to_a(zz, p).wait_send()
+                for aa in range(2):
+                    to_b(zz, aa, p).wait_send()
         return carry
 
     lax.fori_loop(0, Z, z_done, 0)
@@ -365,14 +407,15 @@
     hbm = pl.BlockSpec(memory_space=pl.ANY)
     dma = pltpu.SemaphoreType.DMA
     side = Z if Y * X > 1 else 1
+    pa, pr = parts(D + EXTRA, PA), parts(D, PR)
     return pl.pallas_call(
         functools.partial(body, n),
         out_shape=(
             jax.ShapeDtypeStruct((R, D), BF),
             jax.ShapeDtypeStruct(q_latent.shape, BF),
         ),
-        in_specs=[vmem, vmem, vmem, smem, smem, hbm, hbm, hbm, vmem, vmem, vmem, vmem],
-        out_specs=(vmem, vmem),
+        in_specs=[vmem, vmem, vmem, smem, smem, hbm, hbm, hbm, hbm, vmem, hbm, hbm],
+        out_specs=(vmem, hbm),
         scratch_shapes=[
             pltpu.VMEM((chips, 2, R, D + EXTRA), BF),
             pltpu.VMEM((chips, 2, R, D), BF),
@@ -388,16 +431,25 @@
             pltpu.VMEM((heads * R, 128), F32),
             pltpu.VMEM((n * R, F), F32),
             pltpu.VMEM((n * R, F), F32),
+            pltpu.VMEM(q_latent.shape, BF),
+            pltpu.VMEM(cache_latent.shape, BF),
+            pltpu.VMEM(cache_rope.shape, BF),
+            pltpu.VMEM(q_latent.shape, BF),
             dma((3,)),
-            dma((3, chips)),
-            dma((chips, 2)),
-            dma((Z,)),
-            dma((3, chips)),
-            dma((Z,)),
+            dma((3,)),
+            dma,
+            dma((2, chips, pa)),
+            dma((chips, pa)),
+            dma((2, Z, pa)),
             dma((chips,)),
-            dma((side, 2)),
-            dma((side,)),
-            dma((Z,)),
+            dma((chips,)),
+            dma((2, chips, pr)),
+            dma((Z, pr)),
+            dma((chips,)),
+            dma((chips,)),
+            dma((side, 2, pr)),
+            dma((side, pr)),
+            dma((Z, pr)),
         ],
         compiler_params=pltpu.CompilerParams(
             collective_id=0, has_side_effects=True, vmem_limit_bytes=60 << 20

time: 67.8 us -> 63.3 us (0.934)
  Pallas kernels: 63.5 us -> 58.8 us
    pallas_call x1, Pallas kernels: 63.5 us -> 58.8 us  [per_device(): pl.pallas_call(functools.partial(body, n), out_shape=(jax.ShapeDtypeStruc...]
where the time goes in v3:
time: 63.3 us; the launch traced here: 62.8 us
  Pallas kernels  58.8 us (93%)
  local copies, waits for them, and re-layouts  3.42 us (5%)
  between operations  0.64 us (1%)
    pallas_call x1, Pallas kernels, per_device(): pl.pallas_call(functools.partial(body, n), out_shape=(jax.ShapeDtypeStruc...  58.8 us
    unnamed x2, local copies, waits for them, and re-layouts  3.42 us

profile of v3, /device:TPU:0, one launch (start us, length us, event | category | flops | bytes accessed | tf_op | source)
XLA Modules:
  0.0 62.8 jit_solution(6018257429662397664)
XLA Ops:
  0.6 58.8 %shard_map.131 = (bf16[8,7168]{1,0:T(8,128)(2,1)}, bf16[8,64,512]{2,1,0:T(8,128)(2,1)}) custom-call(bf16[8,7168]{1,0:T(8,128)(2,1)} %normed_ref.1, s32[2,8]{1,0:T(2,128)} %bitcast.2, s32[2,8]{1,0:T(2,128)} %bitcast.3, s32[8]{0:T(128)} %len_ref.1, s32[32]{0:T(128)} %place_ref.1, bf16[1,7168,256]{2,1,0:T(8,128)(2,1)} %wg_hbm.1, bf16[1,7168,256]{2,1,0:T(8,128)(2,1)} %wu_hbm.1, ...), custom_call_target="tpu_custom_call" | custom-call | flops 3000000000 | bytes 13000000 | tf_op jit(solution)/shard_map/pallas_call | solution.py:411
  59.4 1.6 %copy.16 = bf16[8,7168]{1,0:T(8,128)(2,1)} copy(bf16[8,7168]{1,0:T(8,128)(2,1)} %get-tuple-element.4) | data formatting | bytes 229376
  61.0 1.9 %copy.17 = bf16[8,64,512]{2,1,0:T(8,128)(2,1)} copy(bf16[8,64,512]{2,1,0:T(8,128)(2,1)} %get-tuple-element.5) | data formatting | bytes 1048576

commit v4 on v3

--- a/solution.py
+++ b/solution.py
@@ -205,7 +205,7 @@
     for src, dst, s in ((wg_hbm, wg, 0), (wu_hbm, wu, 1), (wd_hbm, wd, 2)):
         pltpu.make_async_copy(src.at[0], dst, w_sem.at[s]).wait()
     rows = n * R
-    kc = 1024
+    kc = 3584
     gacc[...] = jnp.zeros_like(gacc)
     uacc[...] = jnp.zeros_like(uacc)
 
@@ -230,7 +230,7 @@
         coef = coef + jnp.where(info[:, k : k + 1] == mine, route_scale * levels[k] / total, 0.0)
     cf[...] = jnp.broadcast_to(coef, (rows, EXTRA)).reshape(chips, 2, R, EXTRA)
 
-    nc = 1024
+    nc = 1792
 
     def down_half(cc):
         hh = h3[:, cc].reshape(chips * R, F).astype(BF)

time: 63.3 us -> 61.8 us (0.976)
  Pallas kernels: 58.8 us -> 57.2 us
    pallas_call x1, Pallas kernels: 58.8 us -> 57.2 us  [per_device(): pl.pallas_call(functools.partial(body, n), out_shape=(jax.ShapeDtypeStruc...]
where the time goes in v4:
time: 61.8 us; the launch traced here: 61.3 us
  Pallas kernels  57.2 us (93%)
  local copies, waits for them, and re-layouts  3.42 us (6%)
  between operations  0.64 us (1%)
    pallas_call x1, Pallas kernels, per_device(): pl.pallas_call(functools.partial(body, n), out_shape=(jax.ShapeDtypeStruc...  57.2 us
    unnamed x2, local copies, waits for them, and re-layouts  3.42 us

profile of v4, /device:TPU:0, one launch (start us, length us, event | category | flops | bytes accessed | tf_op | source)
XLA Modules:
  0.0 61.3 jit_solution(304781517370256017)
XLA Ops:
  0.6 57.2 %shard_map.131 = (bf16[8,7168]{1,0:T(8,128)(2,1)}, bf16[8,64,512]{2,1,0:T(8,128)(2,1)}) custom-call(bf16[8,7168]{1,0:T(8,128)(2,1)} %normed_ref.1, s32[2,8]{1,0:T(2,128)} %bitcast.2, s32[2,8]{1,0:T(2,128)} %bitcast.3, s32[8]{0:T(128)} %len_ref.1, s32[32]{0:T(128)} %place_ref.1, bf16[1,7168,256]{2,1,0:T(8,128)(2,1)} %wg_hbm.1, bf16[1,7168,256]{2,1,0:T(8,128)(2,1)} %wu_hbm.1, ...), custom_call_target="tpu_custom_call" | custom-call | flops 3000000000 | bytes 13000000 | tf_op jit(solution)/shard_map/pallas_call | solution.py:411
  57.9 1.6 %copy.16 = bf16[8,7168]{1,0:T(8,128)(2,1)} copy(bf16[8,7168]{1,0:T(8,128)(2,1)} %get-tuple-element.4) | data formatting | bytes 229376
  59.4 1.9 %copy.17 = bf16[8,64,512]{2,1,0:T(8,128)(2,1)} copy(bf16[8,64,512]{2,1,0:T(8,128)(2,1)} %get-tuple-element.5) | data formatting | bytes 1048576
